TPU v7x, 32 devices: a whole 2x2x4 slice. The times are simulated.
32 devices in a mesh: groups: 1, pts: 32 (over z, y, x, core).
Axes of the slice: x: 2, y: 2, z: 4, core: 2. Of those that a mesh axis runs over, the one named last changes fastest.
Arguments:
- residual_cols: bfloat16 [16384, 256], P(('groups', 'pts')), may hold values from -6 to 6
- leaf_inverse: bfloat16 [16384, 128], P(('groups', 'pts'))
- basis_left: float32 [7, 16384, 128], P(None, ('groups', 'pts')), may hold values from -0.15625 to 0.15625
- basis_right: float32 [7, 16384, 128], P(None, ('groups', 'pts'))
- point_pos: float32 [16384], replicated, may hold values from 0 to 16, as said below
- map_pos: float32 [2048], P('pts'), may hold values from 0 to 16, as said below
- prior_map: bfloat16 [2048, 256], P(('groups', 'pts')), may hold values from -6 to 6
- block_first: int32 [32, 32], replicated, may hold values from 0 to 2, as said below
- block_count: int32 [32, 32], replicated, may hold values from 0 to 2, as said below
Outputs:
- solved_cols: float32 [16384, 256], P(('groups', 'pts'))
- sample_map: float32 [2048, 256], P(('groups', 'pts'))
Inputs may be any that keep to these rules, and one draw needn't show every extreme that they name: `block_count`: at most 2; the listed blocks of tile d from source s include every block of s that has a point within distance 1 of some map point of tile d; in every draw some tile owner receives 2 blocks from every source; the totals per owner differ strongly between owners. `block_first`: listed blocks stay inside the source's 4 blocks. `point_pos`: points of one leaf block lie in increasing order within an interval of length 1. `map_pos`: the map points of one tile lie within an interval of length at most 6.
All inputs are finite; a program needn't handle non-finite values.
Results may differ from a plain program's by a relative error of at most 0.003.
Values may be sent and summed in bfloat16 or wider, within the bound.
A program may use at most 128 MiB of HBM per device.

v0:
```python
import jax
import jax.numpy as jnp
from jax import lax
from jax.sharding import PartitionSpec as P

LEAF = 128
CAP = 2


amplitude = 0.2
highest = lax.Precision.HIGHEST


def swapped(value, axis, bit):
    mask = 2**bit
    pairs = [(source, source ^ mask) for source in range(lax.axis_size(axis))]
    return lax.ppermute(value, axis, pairs)


def wendland(distance):
    scaled = jnp.minimum(jnp.abs(distance) * (2.0 * LEAF), 1.0)
    return (1.0 - scaled) ** 4 * (1.0 + 4.0 * scaled)


def sibling_sum(projected, depth_bits):
    current = projected
    for bit_index in range(depth_bits):
        current = current + swapped(current, "pts", bit_index)
    received = swapped(current, "pts", depth_bits)
    return received


def body(
    residual_cols,
    leaf_inverse,
    basis_left,
    basis_right,
    point_pos,
    map_pos,
    prior_map,
    block_first,
    block_count,
):
    row_count, samples = residual_cols.shape
    leaf_size = leaf_inverse.shape[1]
    block_local = row_count // leaf_size
    devices = lax.axis_size("pts")
    my_index = lax.axis_index("pts")
    inverses = leaf_inverse.reshape(block_local, leaf_size, leaf_size)
    right_side = residual_cols.reshape(block_local, leaf_size, samples)
    solved = jnp.einsum(
        "bij,bjs->bis", inverses, right_side, preferred_element_type=jnp.float32
    ).reshape(row_count, samples)
    level_total = basis_left.shape[0]
    total_rows = row_count * devices
    for level_index in reversed(range(level_total)):
        half_size = total_rows // 2 ** (level_index + 1)
        left_basis = basis_left[level_index]
        right_basis = basis_right[level_index]
        if half_size < row_count:
            node_count = row_count // (2 * half_size)
            coeff_view = solved.reshape(node_count, 2, half_size, samples)
            right_view = right_basis.reshape(node_count, 2, half_size, -1)
            left_view = left_basis.reshape(node_count, 2, half_size, -1)
            projected = jnp.einsum("nhpr,nhps->nhrs", right_view, coeff_view, precision=highest)
            update = jnp.einsum("nhpr,nhrs->nhps", left_view, projected[:, ::-1], precision=highest)
            solved = solved + update.reshape(row_count, samples)
        else:
            span_devices = half_size // row_count
            depth_bits = span_devices.bit_length() - 1
            projected = jnp.dot(right_basis.T, solved, precision=highest)
            sibling = sibling_sum(projected, depth_bits)
            solved = solved + jnp.dot(left_basis, sibling, precision=highest)
    coeffs = solved.astype(jnp.bfloat16)
    coeff_blocks = coeffs.reshape(block_local, leaf_size, samples)
    map_rows = map_pos.shape[0]
    slot_range = jnp.arange(CAP)[None, :]
    send_first = block_first[:, my_index]
    send_count = block_count[:, my_index]
    send_index = send_first[:, None] + slot_range
    send_live = slot_range < send_count[:, None]
    outgoing = jnp.where(
        send_live[:, :, None, None], coeff_blocks[send_index], jnp.zeros((), jnp.bfloat16)
    )
    sources = jnp.arange(devices)[:, None]
    slot_index = block_first[my_index][:, None] + slot_range
    live = slot_range < block_count[my_index][:, None]
    point_index = (sources * block_local + slot_index)[:, :, None] * leaf_size + jnp.arange(
        leaf_size
    )
    positions = point_pos[point_index]
    kernel = amplitude * wendland(map_pos[:, None, None, None] - positions[None])
    weights = (
        jnp.where(live[None, :, :, None], kernel, 0.0).astype(jnp.bfloat16).reshape(map_rows, -1)
    )
    mapped = jnp.dot(
        weights,
        lax.all_to_all(outgoing, "pts", split_axis=0, concat_axis=0, tiled=True).reshape(
            weights.shape[1], -1
        ),
        preferred_element_type=jnp.float32,
    )
    sample_map = prior_map.astype(jnp.float32) + mapped
    return (solved, sample_map)


def solution(mesh):
    in_specs = (
        P(("groups", "pts"), None),
        P(("groups", "pts"), None),
        P(None, ("groups", "pts"), None),
        P(None, ("groups", "pts"), None),
        P(),
        P("pts"),
        P(("groups", "pts"), None),
        P(),
        P(),
    )
    out_specs = (P(("groups", "pts"), None), P(("groups", "pts"), None))
    return jax.shard_map(body, mesh=mesh, in_specs=in_specs, out_specs=out_specs, check_vma=False)
```

profile of v0, /device:TPU:0, one launch (start us, length us, event | category | flops | bytes accessed | tf_op | source)
XLA Modules:
  0.0 193.6 jit_solution(8209846204342725354)
XLA Ops:
  0.6 1.1 fusion.42
  1.8 1.1 fusion.44
  2.9 0.7 convolution_bitcast_fusion.5
  3.6 1.1 fusion.41
  4.7 0.6 fusion.45
  5.4 0.6 convolution_bitcast_fusion.6
  6.0 0.6 bitcast_add_fusion.1
  6.7 2.0 %convolution_bitcast_fusion.11 = f32[128,256]{0,1:T(8,128)S(1)} fusion(f32[512,256]{1,0:T(8,128)S(1)} %bitcast.132, f32[7,512,128]{2,1,0:T(8,128)} %param.12), kind=kOutput, calls=%fused_computation.20 | convolution fusion | flops 201326592 | bytes 917504 | tf_op jit(solution)/shard_map/dot_general | solution.py:71
  10.2 1.8 fusion
  11.9 0.6 convolution_bitcast_fusion.10
  12.8 1.2 collective-permute-done.1
  14.0 2.7 %collective-permute-start.2 = (f32[128,256]{0,1:T(8,128)S(1)}, f32[128,256]{0,1:T(8,128)S(1)}, u32[]{:S(2)}, u32[]{:S(2)}) collective-permute-start(f32[128,256]{0,1:T(8,128)S(1)} %add.174), channel_id=1, source_target_pairs={{0,2},{1,3},{2,0},{3,1},{4,6},{5,7},{6,4},{7,5},{8,10},{9,11},{10,... | collective-permute-start | bytes 393224 | tf_op jit(solution)/shard_map/ppermute | solution.py:17
  16.7 4.0 %collective-permute-done.2 = f32[128,256]{0,1:T(8,128)S(1)} collective-permute-done((f32[128,256]{0,1:T(8,128)S(1)}, f32[128,256]{0,1:T(8,128)S(1)}, u32[]{:S(2)}, u32[]{:S(2)}) %collective-permute-start.2) | collective-permute-done | bytes 131104 | tf_op jit(solution)/shard_map/ppermute | solution.py:17
  20.7 1.5 fusion.1
  22.2 0.6 convolution_bitcast_fusion.9
  22.9 1.3 collective-permute-done.3
  24.2 1.8 collective-permute-start.4
  26.1 3.8 %collective-permute-done.4 = f32[128,256]{0,1:T(8,128)S(1)} collective-permute-done((f32[128,256]{0,1:T(8,128)S(1)}, f32[128,256]{0,1:T(8,128)S(1)}, u32[]{:S(2)}, u32[]{:S(2)}) %collective-permute-start.4) | collective-permute-done | bytes 131104 | tf_op jit(solution)/shard_map/ppermute | solution.py:17
  29.9 1.8 collective-permute-start.5
  31.7 3.2 %collective-permute-done.5 = f32[128,256]{0,1:T(8,128)S(1)} collective-permute-done((f32[128,256]{0,1:T(8,128)S(1)}, f32[128,256]{0,1:T(8,128)S(1)}, u32[]{:S(2)}, u32[]{:S(2)}) %collective-permute-start.5) | collective-permute-done | bytes 131104 | tf_op jit(solution)/shard_map/ppermute | solution.py:17
  34.9 1.5 fusion.2
  36.5 0.6 convolution_bitcast_fusion.8
  37.1 1.3 collective-permute-done.6
  38.5 1.8 collective-permute-start.7
  40.3 3.8 %collective-permute-done.7 = f32[128,256]{0,1:T(8,128)S(1)} collective-permute-done((f32[128,256]{0,1:T(8,128)S(1)}, f32[128,256]{0,1:T(8,128)S(1)}, u32[]{:S(2)}, u32[]{:S(2)}) %collective-permute-start.7) | collective-permute-done | bytes 131104 | tf_op jit(solution)/shard_map/ppermute | solution.py:17
  44.1 1.8 collective-permute-start.8
  46.0 3.2 %collective-permute-done.8 = f32[128,256]{0,1:T(8,128)S(1)} collective-permute-done((f32[128,256]{0,1:T(8,128)S(1)}, f32[128,256]{0,1:T(8,128)S(1)}, u32[]{:S(2)}, u32[]{:S(2)}) %collective-permute-start.8) | collective-permute-done | bytes 131104 | tf_op jit(solution)/shard_map/ppermute | solution.py:17
  49.2 1.9 collective-permute-start.9
  51.1 3.1 %collective-permute-done.9 = f32[128,256]{0,1:T(8,128)S(1)} collective-permute-done((f32[128,256]{0,1:T(8,128)S(1)}, f32[128,256]{0,1:T(8,128)S(1)}, u32[]{:S(2)}, u32[]{:S(2)}) %collective-permute-start.9) | collective-permute-done | bytes 131104 | tf_op jit(solution)/shard_map/ppermute | solution.py:17
  54.2 1.5 fusion.3
  56.4 1.3 collective-permute-done.10
  57.8 1.8 collective-permute-start.11
  59.6 3.8 %collective-permute-done.11 = f32[128,256]{0,1:T(8,128)S(1)} collective-permute-done((f32[128,256]{0,1:T(8,128)S(1)}, f32[128,256]{0,1:T(8,128)S(1)}, u32[]{:S(2)}, u32[]{:S(2)}) %collective-permute-start.11) | collective-permute-done | bytes 131104 | tf_op jit(solution)/shard_map/ppermute | solution.py:17
  63.4 1.8 collective-permute-start.12
  65.4 3.0 %collective-permute-done.12 = f32[128,256]{0,1:T(8,128)S(1)} collective-permute-done((f32[128,256]{0,1:T(8,128)S(1)}, f32[128,256]{0,1:T(8,128)S(1)}, u32[]{:S(2)}, u32[]{:S(2)}) %collective-permute-start.12) | collective-permute-done | bytes 131104 | tf_op jit(solution)/shard_map/ppermute | solution.py:17
  68.5 1.9 collective-permute-start.13
  70.4 3.1 %collective-permute-done.13 = f32[128,256]{0,1:T(8,128)S(1)} collective-permute-done((f32[128,256]{0,1:T(8,128)S(1)}, f32[128,256]{0,1:T(8,128)S(1)}, u32[]{:S(2)}, u32[]{:S(2)}) %collective-permute-start.13) | collective-permute-done | bytes 131104 | tf_op jit(solution)/shard_map/ppermute | solution.py:17
  73.5 3.3 %collective-permute-start.14 = (f32[128,256]{0,1:T(8,128)S(1)}, f32[128,256]{0,1:T(8,128)S(1)}, u32[]{:S(2)}, u32[]{:S(2)}) collective-permute-start(f32[128,256]{0,1:T(8,128)S(1)} %add.186), channel_id=1, source_target_pairs={{0,16},{1,17},{2,18},{3,19},{4,20},{5,21},{6,22},{7,23},{8,24},{9,... | collective-permute-start | bytes 393224 | tf_op jit(solution)/shard_map/ppermute | solution.py:17
  77.1 4.2 %collective-permute-done.14 = f32[128,256]{0,1:T(8,128)S(1)} collective-permute-done((f32[128,256]{0,1:T(8,128)S(1)}, f32[128,256]{0,1:T(8,128)S(1)}, u32[]{:S(2)}, u32[]{:S(2)}) %collective-permute-start.14) | collective-permute-done | bytes 131104 | tf_op jit(solution)/shard_map/ppermute | solution.py:17
  81.2 1.5 fusion.43
  82.9 2.8 %gather_fusion.1 = bf16[64,128,256]{2,1,0:T(8,128)(2,1)} fusion(bf16[4,128,256]{2,1,0:T(8,128)(2,1)S(1)} %bitcast.126, s32[1024]{0:T(1024)S(1)} %pad_clamp_fusion), kind=kCustom, calls=%fused_computation.1 | custom fusion | bytes 8388864 | tf_op jit(solution)/shard_map/gather | solution.py:83
  85.7 4.5 %broadcast_select_fusion = bf16[32,2,128,256]{3,2,1,0:T(8,128)(2,1)} fusion(bf16[32,2,128,256]{3,2,1,0:T(8,128)(2,1)} %bitcast.127, pred[32,2]{1,0:T(8,128)(4,1)S(1)} %iota_compare_fusion), kind=kLoop, calls=%fused_computation.2 | loop fusion | flops 2097152 | bytes 8388672 | tf_op jit(solution)/shard_map/jit(_where)/select_n | solution.py:82
  90.2 5.9 %all-to-all-start = ((bf16[32,2,128,256]{3,2,1,0:T(8,128)(2,1)}), bf16[32,2,128,256]{3,2,1,0:T(8,128)(2,1)}, u32[]{:S(2)}, u32[]{:S(2)}) async-start(bf16[32,2,128,256]{3,2,1,0:T(8,128)(2,1)} %broadcast_select_fusion), calls=%async_computation | async-start | bytes 8388608 | tf_op jit(solution)/shard_map/all_to_all | solution.py:98
  96.3 0.6 copy-done.1
  96.9 45.5 %gather_fusion = f32[8192]{0:T(1024)S(1)} fusion(f32[16384]{0:T(1024)S(1)} %copy-done.1, s32[8192]{0:T(1024)S(1)} %broadcast_clamp_fusion), kind=kCustom, calls=%fused_computation | custom fusion | bytes 98304 | tf_op jit(solution)/shard_map/gather | solution.py:91
  142.5 1.0 copy.20
  143.5 46.2 %all-to-all-done = bf16[32,2,128,256]{3,2,1,0:T(8,128)(2,1)} async-done(((bf16[32,2,128,256]{3,2,1,0:T(8,128)(2,1)}), bf16[32,2,128,256]{3,2,1,0:T(8,128)(2,1)}, u32[]{:S(2)}, u32[]{:S(2)}) %all-to-all-start) | async-done | bytes 4194336 | tf_op jit(solution)/shard_map/all_to_all | solution.py:98
  189.8 3.8 %fusion.5 = f32[64,256]{1,0:T(8,128)} fusion(bf16[32,2,128,256]{3,2,1,0:T(8,128)(2,1)} %all-to-all-done, f32[32,2,128]{2,1,0:T(2,128)S(1)} %bitcast.140, f32[64]{0:T(128)S(1)} %copy-done.6, pred[32,2]{1,0:T(8,128)(4,1)S(1)} %iota_compare_fusion.1, bf16[64,256]{1,0:T(8,128)(2,1)S(1)} %copy-done.5), kind=kOutput, calls=%fused_computation.22 | convolution fusion | flops 275283968 | bytes 4325696 | tf_op jit(solution)/shard_map/dot_general | solution.py:96
  (49 shorter events, 3.7 us)
Async XLA Ops:
  0.6 1.1 copy-start
  8.6 1.5 collective-permute-start
  9.8 2.1 %copy-start.2 = (f32[7,512,128]{2,1,0:T(8,128)S(1)}, f32[7,512,128]{2,1,0:T(8,128)}, u32[]{:S(2)}) copy-start(f32[7,512,128]{2,1,0:T(8,128)} %param.12) | copy-start | bytes 5505028
  12.5 1.4 collective-permute-start.1
  14.0 6.7 %collective-permute-start.2 = (f32[128,256]{0,1:T(8,128)S(1)}, f32[128,256]{0,1:T(8,128)S(1)}, u32[]{:S(2)}, u32[]{:S(2)}) collective-permute-start(f32[128,256]{0,1:T(8,128)S(1)} %add.174), channel_id=1, source_target_pairs={{0,2},{1,3},{2,0},{3,1},{4,6},{5,7},{6,4},{7,5},{8,10},{9,11},{10,... | collective-permute-start | bytes 393224 | tf_op jit(solution)/shard_map/ppermute | solution.py:17
  22.8 1.4 collective-permute-start.3
  24.2 5.6 %collective-permute-start.4 = (f32[128,256]{0,1:T(8,128)S(1)}, f32[128,256]{0,1:T(8,128)S(1)}, u32[]{:S(2)}, u32[]{:S(2)}) collective-permute-start(f32[128,256]{0,1:T(8,128)S(1)} %add.176), channel_id=1, source_target_pairs={{0,2},{1,3},{2,0},{3,1},{4,6},{5,7},{6,4},{7,5},{8,10},{9,11},{10,... | collective-permute-start | bytes 393224 | tf_op jit(solution)/shard_map/ppermute | solution.py:17
  29.9 5.0 %collective-permute-start.5 = (f32[128,256]{0,1:T(8,128)S(1)}, f32[128,256]{0,1:T(8,128)S(1)}, u32[]{:S(2)}, u32[]{:S(2)}) collective-permute-start(f32[128,256]{0,1:T(8,128)S(1)} %add.177), channel_id=1, source_target_pairs={{0,4},{1,5},{2,6},{3,7},{4,0},{5,1},{6,2},{7,3},{8,12},{9,13},{10,... | collective-permute-start | bytes 393224 | tf_op jit(solution)/shard_map/ppermute | solution.py:17
  37.0 28.2 %copy-start.3 = (s32[32,32]{1,0:T(8,128)S(1)}, s32[32,32]{1,0:T(8,128)}, u32[]{:S(2)}) copy-start(s32[32,32]{1,0:T(8,128)} %param.16) | copy-start | bytes 12292
  37.1 28.2 %copy-start.4 = (s32[32,32]{1,0:T(8,128)S(1)}, s32[32,32]{1,0:T(8,128)}, u32[]{:S(2)}) copy-start(s32[32,32]{1,0:T(8,128)} %param.17) | copy-start | bytes 12292
  37.1 1.4 collective-permute-start.6
  38.5 5.6 %collective-permute-start.7 = (f32[128,256]{0,1:T(8,128)S(1)}, f32[128,256]{0,1:T(8,128)S(1)}, u32[]{:S(2)}, u32[]{:S(2)}) collective-permute-start(f32[128,256]{0,1:T(8,128)S(1)} %add.179), channel_id=1, source_target_pairs={{0,2},{1,3},{2,0},{3,1},{4,6},{5,7},{6,4},{7,5},{8,10},{9,11},{10,... | collective-permute-start | bytes 393224 | tf_op jit(solution)/shard_map/ppermute | solution.py:17
  44.1 5.0 %collective-permute-start.8 = (f32[128,256]{0,1:T(8,128)S(1)}, f32[128,256]{0,1:T(8,128)S(1)}, u32[]{:S(2)}, u32[]{:S(2)}) collective-permute-start(f32[128,256]{0,1:T(8,128)S(1)} %add.180), channel_id=1, source_target_pairs={{0,4},{1,5},{2,6},{3,7},{4,0},{5,1},{6,2},{7,3},{8,12},{9,13},{10,... | collective-permute-start | bytes 393224 | tf_op jit(solution)/shard_map/ppermute | solution.py:17
  49.2 5.0 %collective-permute-start.9 = (f32[128,256]{0,1:T(8,128)S(1)}, f32[128,256]{0,1:T(8,128)S(1)}, u32[]{:S(2)}, u32[]{:S(2)}) collective-permute-start(f32[128,256]{0,1:T(8,128)S(1)} %add.181), channel_id=1, source_target_pairs={{0,8},{1,9},{2,10},{3,11},{4,12},{5,13},{6,14},{7,15},{8,0},{9,1},... | collective-permute-start | bytes 393224 | tf_op jit(solution)/shard_map/ppermute | solution.py:17
  56.3 1.4 collective-permute-start.10
  57.8 5.6 %collective-permute-start.11 = (f32[128,256]{0,1:T(8,128)S(1)}, f32[128,256]{0,1:T(8,128)S(1)}, u32[]{:S(2)}, u32[]{:S(2)}) collective-permute-start(f32[128,256]{0,1:T(8,128)S(1)} %add.183), channel_id=1, source_target_pairs={{0,2},{1,3},{2,0},{3,1},{4,6},{5,7},{6,4},{7,5},{8,10},{9,11},{10,... | collective-permute-start | bytes 393224 | tf_op jit(solution)/shard_map/ppermute | solution.py:17
  63.4 5.0 %collective-permute-start.12 = (f32[128,256]{0,1:T(8,128)S(1)}, f32[128,256]{0,1:T(8,128)S(1)}, u32[]{:S(2)}, u32[]{:S(2)}) collective-permute-start(f32[128,256]{0,1:T(8,128)S(1)} %add.184), channel_id=1, source_target_pairs={{0,4},{1,5},{2,6},{3,7},{4,0},{5,1},{6,2},{7,3},{8,12},{9,13},{10,... | collective-permute-start | bytes 393224 | tf_op jit(solution)/shard_map/ppermute | solution.py:17
  68.5 5.0 %collective-permute-start.13 = (f32[128,256]{0,1:T(8,128)S(1)}, f32[128,256]{0,1:T(8,128)S(1)}, u32[]{:S(2)}, u32[]{:S(2)}) collective-permute-start(f32[128,256]{0,1:T(8,128)S(1)} %add.185), channel_id=1, source_target_pairs={{0,8},{1,9},{2,10},{3,11},{4,12},{5,13},{6,14},{7,15},{8,0},{9,1},... | collective-permute-start | bytes 393224 | tf_op jit(solution)/shard_map/ppermute | solution.py:17
  73.5 7.7 %collective-permute-start.14 = (f32[128,256]{0,1:T(8,128)S(1)}, f32[128,256]{0,1:T(8,128)S(1)}, u32[]{:S(2)}, u32[]{:S(2)}) collective-permute-start(f32[128,256]{0,1:T(8,128)S(1)} %add.186), channel_id=1, source_target_pairs={{0,16},{1,17},{2,18},{3,19},{4,20},{5,21},{6,22},{7,23},{8,24},{9,... | collective-permute-start | bytes 393224 | tf_op jit(solution)/shard_map/ppermute | solution.py:17
  90.2 99.6 %all-to-all-start = ((bf16[32,2,128,256]{3,2,1,0:T(8,128)(2,1)}), bf16[32,2,128,256]{3,2,1,0:T(8,128)(2,1)}, u32[]{:S(2)}, u32[]{:S(2)}) async-start(bf16[32,2,128,256]{3,2,1,0:T(8,128)(2,1)} %broadcast_select_fusion), calls=%async_computation | async-start | bytes 8388608 | tf_op jit(solution)/shard_map/all_to_all | solution.py:98
  96.1 0.8 copy-start.1
  96.9 92.9 %copy-start.5 = (bf16[64,256]{1,0:T(8,128)(2,1)S(1)}, bf16[64,256]{1,0:T(8,128)(2,1)}, u32[]{:S(2)}) copy-start(bf16[64,256]{1,0:T(8,128)(2,1)} %param.15) | copy-start | bytes 98308
  96.9 92.9 %copy-start.6 = (f32[64]{0:T(128)S(1)}, f32[64]{0:T(128)}, u32[]{:S(2)}) copy-start(f32[64]{0:T(128)} %param.14) | copy-start | bytes 772
where the time goes:
time: 194 us
  waiting for transfers between devices  86.9 us (45%)
  local copies, waits for them, and re-layouts  53.2 us (27%)
  starting transfers between devices  27.7 us (14%)
  matrix products  19.7 us (10%)
  other arithmetic  5.1 us (3%)
    all_to_all x1, waiting for transfers between devices, body(): lax.all_to_all(outgoing, 'pts', split_axis=0, concat_axis=0, tiled=True)  46.2 us
    gather x1, local copies, waits for them, and re-layouts, body(): positions = point_pos[point_index]  45.5 us
    ppermute x15, waiting for transfers between devices, swapped(): return lax.ppermute(value, axis, pairs)  40.7 us
    ppermute x15, starting transfers between devices, swapped(): return lax.ppermute(value, axis, pairs)  21.8 us
    dot_general x5, matrix products, body(): solved = solved + jnp.dot(left_basis, sibling, precision=highest)  7.89 us
    all_to_all x1, starting transfers between devices, body(): lax.all_to_all(outgoing, 'pts', split_axis=0, concat_axis=0, tiled=True)  5.87 us
    select_n x1, other arithmetic, body(): jnp.where(send_live[:, :, None, None], coeff_blocks[send_index], jnp.zero...  4.46 us
    dot_general x5, matrix products, body(): projected = jnp.dot(right_basis.T, solved, precision=highest)  4.29 us
  transfers between devices with their start and end apart: 16, of which 16 were waited for; matrix products, arithmetic and copies ran while one was open for 25% of the time, Pallas kernels for 0%

commit v1 on v0

v1 whole, which is shorter than its diff:
```python
import functools

import jax
import jax.numpy as jnp
from jax import lax
from jax.experimental import pallas as pl
from jax.experimental.pallas import tpu as pltpu
from jax.sharding import PartitionSpec as P

AMPLITUDE = 0.2
FAR = -1e6
f32 = jnp.float32
bf16 = jnp.bfloat16


def split(value):
    high = value.astype(bf16)
    return high, (value - high.astype(f32)).astype(bf16)


def mm(a, b):
    return jnp.dot(a, b, preferred_element_type=f32)


def mm3(a, b):
    return mm(a[0], b[0]) + mm(a[0], b[1]) + mm(a[1], b[0])


def kernel(
    n,
    leaf,
    res_ref,
    inv_ref,
    bl_ref,
    br_ref,
    pp_ref,
    mp_ref,
    prior_ref,
    first_ref,
    count_ref,
    out_ref,
    map_ref,
    xs,
    rth,
    rtl,
    lh,
    ll,
    gf,
    gs,
    gr,
    tf,
    ts,
    tr,
    cbuf,
    co,
    mpb,
    wts,
    acc,
    ms,
    mr,
    send_sem,
    recv_sem,
):
    rows, samples = res_ref.shape
    rank = bl_ref.shape[2]
    levels = bl_ref.shape[0]
    half = samples // 2
    depth = n.bit_length() - 1
    tile = prior_ref.shape[0]
    me = lax.axis_index("pts")
    bits = [lax.rem(me // 2**k, 2) for k in range(depth)]
    partners = [me + 2**k * (1 - 2 * bits[k]) for k in range(depth)]
    par = bits[0]
    started = []

    def remote(src, dst, k):
        index = len(started)
        copy = pltpu.make_async_remote_copy(
            src_ref=src,
            dst_ref=dst,
            send_sem=send_sem.at[index],
            recv_sem=recv_sem.at[index],
            device_id={"pts": partners[k]},
            device_id_type=pl.DeviceIdType.MESH,
        )
        copy.start()
        started.append(copy)
        return copy

    barrier = pltpu.get_barrier_semaphore()
    for k in range(depth):
        pl.semaphore_signal(
            barrier, inc=1, device_id={"pts": partners[k]}, device_id_type=pl.DeviceIdType.MESH
        )

    pairs = [m * (m + 1) // 2 for m in range(depth)]
    g_off, t_off, m_off = [], [], []
    g_at = t_at = m_at = 0
    for k in range(depth):
        m = depth - 1 - k
        g_off.append(g_at)
        t_off.append(t_at)
        m_off.append(m_at)
        g_at += pairs[m]
        t_at += m + 1
        m_at += n // 2 ** (k + 1) * tile

    mpb[0] = mp_ref[0]
    for l in range(depth):
        high, low = split(br_ref[l].T)
        rth[l * rank : (l + 1) * rank, :] = high
        rtl[l * rank : (l + 1) * rank, :] = low
        high, low = split(bl_ref[l])
        lh[:, l * rank : (l + 1) * rank] = high
        ll[:, l * rank : (l + 1) * rank] = low
    at = 0
    for m in range(depth - 1, 0, -1):
        product = mm(rth[: m * rank, :], lh[:, m * rank : (m + 1) * rank])
        product = product.reshape(m, rank, rank)
        gf[at : at + m] = product
        gs[at : at + m] = product.astype(bf16)
        at += m

    pl.semaphore_wait(barrier, depth)

    def start_g(k):
        size = pairs[depth - 1 - k]
        view = pl.ds(g_off[k], size)
        return remote(gs.at[view], gr.at[view], k)

    def start_mp(k):
        return remote(mpb.at[pl.ds(0, 2**k)], mpb.at[pl.ds(2**k, 2**k)], k)

    mp_copy = start_mp(0)
    g_copy = start_g(0) if depth > 1 else None

    for b in range(rows // leaf):
        part = mm(inv_ref[b * leaf : (b + 1) * leaf, :], res_ref[b * leaf : (b + 1) * leaf, :])
        xs[b * leaf : (b + 1) * leaf, :] = part
    total_rows = rows * n
    for level in range(levels - 1, depth - 1, -1):
        size = total_rows // 2 ** (level + 1)
        count = rows // size
        projected = []
        for a in range(count):
            view = slice(a * size, (a + 1) * size)
            projected.append(split(mm3(split(br_ref[level, view, :].T), split(xs[view, :]))))
        for a in range(count):
            view = slice(a * size, (a + 1) * size)
            xs[view, :] += mm3(split(bl_ref[level, view, :]), projected[a ^ 1])

    mp_copy.wait_recv()
    mp_next = 1
    if mp_next < depth:
        mp_copy = start_mp(mp_next)

    for h in range(2):
        x_high, x_low = split(xs[:, h * half : (h + 1) * half])
        t_all = mm(rth[...], x_high) + mm(rth[...], x_low) + mm(rtl[...], x_high)
        t_all = t_all.reshape(depth, rank, half)
        tf[h] = t_all
        ts[h, pl.ds(0, depth)] = t_all.astype(bf16)

    own_u = pp_ref[me]

    def weights(low_e, high_e):
        def one(e, carry):
            spot = 0
            other = 0
            for i in range(depth):
                bit = lax.rem(e // 2**i, 2)
                spot = spot + bit * 2 ** (depth - 1 - i)
                other = other + lax.rem(bit + bits[i], 2) * 2**i
            first = first_ref[other, me]
            last = first + count_ref[other, me]
            t_col = jnp.broadcast_to(mpb[e], (128, 128)).T[:tile]
            base = pl.multiple_of(spot * tile, tile)
            for b in range(rows // leaf):
                u_row = own_u[:, b * leaf : (b + 1) * leaf]
                listed = jnp.logical_and(first <= b, b < last)
                u_row = jnp.where(listed, u_row, FAR)
                scaled = jnp.minimum(jnp.abs(t_col - u_row) * (2.0 * leaf), 1.0)
                rest = 1.0 - scaled
                square = rest * rest
                value = AMPLITUDE * (square * square * (1.0 + 4.0 * scaled))
                wts[pl.ds(base, tile), b * leaf : (b + 1) * leaf] = value.astype(bf16)
            return carry

        lax.fori_loop(low_e, high_e, one, 0)

    forwards = []
    for k in range(depth):
        m = depth - 1 - k
        span = pl.ds(t_off[k], m + 1)
        if k == 0:
            t_copies = [
                remote(ts.at[1 - par, span], tr.at[span], 0),
                remote(ts.at[par, m], cbuf.at[m, par], 0),
            ]
        else:
            t_copies = [remote(ts.at[par, span], tr.at[span], k)]
        if mp_next < depth:
            mp_copy.wait_recv()
            mp_next += 1
            if mp_next < depth:
                mp_copy = start_mp(mp_next)
        if m > 0:
            g_copy.wait_recv()
            rest = pairs[m] - m
            if rest > 0:
                total = gf[g_off[k] + m : g_off[k] + pairs[m]] + gr[
                    g_off[k] + m : g_off[k] + pairs[m]
                ].astype(f32)
                gf[g_off[k + 1] : g_off[k + 1] + rest] = total
                gs[g_off[k + 1] : g_off[k + 1] + rest] = total.astype(bf16)
                g_copy = start_g(k + 1)
        if k == depth - 2:
            while mp_next < depth:
                mp_copy.wait_recv()
                mp_next += 1
                if mp_next < depth:
                    mp_copy = start_mp(mp_next)
            weights(0, n // 2)
        if k == depth - 1:
            weights(n // 2, n)
        for copy in t_copies:
            copy.wait_recv()
        if k > 0:
            forwards.append(remote(tr.at[t_off[k] + m], cbuf.at[m, par], 0))
        if m > 0:
            mine = ts[par, t_off[k] + m]
            theirs = tr[t_off[k] + m]
            g_mine = gs[g_off[k] : g_off[k] + m].reshape(m * rank, rank)
            g_theirs = gr[g_off[k] : g_off[k] + m].reshape(m * rank, rank)
            gained = mm(g_mine, theirs) + mm(g_theirs, mine)
            total = (
                tf[par, :m]
                + tr[t_off[k] : t_off[k] + m].astype(f32)
                + gained.reshape(m, rank, half)
            )
            tf[par, pl.ds(0, m)] = total
            ts[par, pl.ds(t_off[k + 1], m)] = total.astype(bf16)

    mine_cols = pl.ds(pl.multiple_of(par * half, half), half)
    other_cols = pl.ds(pl.multiple_of((1 - par) * half, half), half)

    def finish(columns, parts):
        stacked = jnp.concatenate(parts, axis=0)
        total = xs[:, columns] + mm(lh[...], stacked) + mm(ll[...], stacked)
        out_ref[:, columns] = total
        co[:, columns] = total.astype(bf16)

    finish(mine_cols, [tr[t_off[depth - 1 - m] + m] for m in range(depth)])
    for copy in forwards:
        copy.wait_recv()
    finish(other_cols, [cbuf[m, 1 - par] for m in range(depth)])

    step_rows = min(256, n // 2 * tile)
    half_rows = n // 2 * tile

    def send_part(i, carry):
        at = pl.multiple_of(i * step_rows, step_rows)
        ms[pl.ds(at, step_rows), :] = mm(
            wts[pl.ds(half_rows + at, step_rows), :], co[...]
        ).astype(bf16)
        return carry

    def keep_part(i, carry):
        at = pl.multiple_of(i * step_rows, step_rows)
        acc[pl.ds(at, step_rows), :] = mm(wts[pl.ds(at, step_rows), :], co[...])
        return carry

    lax.fori_loop(0, half_rows // step_rows, send_part, 0)
    copy = remote(ms.at[pl.ds(0, half_rows)], mr.at[pl.ds(0, half_rows)], 0)
    lax.fori_loop(0, half_rows // step_rows, keep_part, 0)
    for k in range(1, depth):
        size = n // 2 ** (k + 1) * tile
        copy.wait_recv()
        old = m_off[k - 1]
        ms[m_off[k] : m_off[k] + size, :] = (
            acc[size : 2 * size, :] + mr[old + size : old + 2 * size, :].astype(f32)
        ).astype(bf16)
        copy = remote(ms.at[pl.ds(m_off[k], size)], mr.at[pl.ds(m_off[k], size)], k)
        acc[:size, :] += mr[old : old + size, :].astype(f32)
    partial = prior_ref[...].astype(f32) + acc[:tile, :]
    copy.wait_recv()
    old = m_off[depth - 1]
    map_ref[...] = partial + mr[old : old + tile, :].astype(f32)
    for copy in started:
        copy.wait_send()


def body(
    residual_cols,
    leaf_inverse,
    basis_left,
    basis_right,
    point_pos,
    map_pos,
    prior_map,
    block_first,
    block_count,
):
    rows, samples = residual_cols.shape
    leaf = leaf_inverse.shape[1]
    levels, _, rank = basis_left.shape
    n = lax.axis_size("pts")
    depth = n.bit_length() - 1
    tile = map_pos.shape[0]
    half = samples // 2
    pair_total = sum(m * (m + 1) // 2 for m in range(depth))
    t_total = depth * (depth + 1) // 2
    vmem = pl.BlockSpec(memory_space=pltpu.VMEM)
    smem = pl.BlockSpec(memory_space=pltpu.SMEM)
    copies = 5 * depth
    return pl.pallas_call(
        functools.partial(kernel, n, leaf),
        out_shape=(
            jax.ShapeDtypeStruct((rows, samples), f32),
            jax.ShapeDtypeStruct((tile, samples), f32),
        ),
        in_specs=[vmem] * 7 + [smem] * 2,
        out_specs=(vmem, vmem),
        scratch_shapes=[
            pltpu.VMEM((rows, samples), f32),
            pltpu.VMEM((depth * rank, rows), bf16),
            pltpu.VMEM((depth * rank, rows), bf16),
            pltpu.VMEM((rows, depth * rank), bf16),
            pltpu.VMEM((rows, depth * rank), bf16),
            pltpu.VMEM((pair_total, rank, rank), f32),
            pltpu.VMEM((pair_total, rank, rank), bf16),
            pltpu.VMEM((pair_total, rank, rank), bf16),
            pltpu.VMEM((2, depth, rank, half), f32),
            pltpu.VMEM((2, t_total, rank, half), bf16),
            pltpu.VMEM((t_total, rank, half), bf16),
            pltpu.VMEM((depth, 2, rank, half), bf16),
            pltpu.VMEM((rows, samples), bf16),
            pltpu.VMEM((n, 1, 128), f32),
            pltpu.VMEM((n * tile, rows), bf16),
            pltpu.VMEM((n // 2 * tile, samples), f32),
            pltpu.VMEM((n * tile, samples), bf16),
            pltpu.VMEM((n * tile, samples), bf16),
            pltpu.SemaphoreType.DMA((copies,)),
            pltpu.SemaphoreType.DMA((copies,)),
        ],
        compiler_params=pltpu.CompilerParams(
            collective_id=0, has_side_effects=True, vmem_limit_bytes=60 * 1024 * 1024
        ),
    )(
        residual_cols,
        leaf_inverse,
        basis_left,
        basis_right,
        point_pos.reshape(n, 1, rows),
        jnp.pad(map_pos, (0, 128 - tile)).reshape(1, 1, 128),
        prior_map,
        block_first,
        block_count,
    )


def solution(mesh):
    in_specs = (
        P(("groups", "pts"), None),
        P(("groups", "pts"), None),
        P(None, ("groups", "pts"), None),
        P(None, ("groups", "pts"), None),
        P(),
        P("pts"),
        P(("groups", "pts"), None),
        P(),
        P(),
    )
    out_specs = (P(("groups", "pts"), None), P(("groups", "pts"), None))
    return jax.shard_map(body, mesh=mesh, in_specs=in_specs, out_specs=out_specs, check_vma=False)
```

time: 194 us -> 58.3 us (0.30)
  waiting for transfers between devices: 86.9 us -> 0 us
  Pallas kernels: 0 us -> 53 us
  local copies, waits for them, and re-layouts: 53.2 us -> 4.51 us
  starting transfers between devices: 27.7 us -> 0 us
  matrix products: 19.7 us -> 0 us
  other arithmetic: 5.1 us -> 0 us
    pallas_call x0 -> x1, Pallas kernels: none -> 53 us  [body(): pl.pallas_call(functools.partial(kernel, n, leaf), out_shape=(jax.ShapeDt...]
    gather x2 -> x0, local copies, waits for them, and re-layouts: 48.3 us -> none  [the longest x1 45.5 us: body(): positions = point_pos[point_index]]
    all_to_all x1 -> x0, waiting for transfers between devices: 46.2 us -> none  [body(): lax.all_to_all(outgoing, 'pts', split_axis=0, concat_axis=0, tiled=True)]
    ppermute x15 -> x0, waiting for transfers between devices: 40.7 us -> none  [swapped(): return lax.ppermute(value, axis, pairs)]
    ppermute x15 -> x0, starting transfers between devices: 21.8 us -> none  [swapped(): return lax.ppermute(value, axis, pairs)]
    dot_general x16 -> x0, matrix products: 19.7 us -> none  [the longest x5 7.89 us: body(): solved = solved + jnp.dot(left_basis, sibling, precision=highest)]
    all_to_all x1 -> x0, starting transfers between devices: 5.87 us -> none  [body(): lax.all_to_all(outgoing, 'pts', split_axis=0, concat_axis=0, tiled=True)]
    select_n x3 -> x0, other arithmetic: 4.64 us -> none  [the longest x1 4.46 us: body(): jnp.where(send_live[:, :, None, None], coeff_blocks[send_index], jnp.zero...]
  transfers between devices with their start and end apart: 16 -> 0, of which waited for: 16 -> 0; matrix products, arithmetic and copies ran while one was open for 25% -> 0% of each run, Pallas kernels for 0% -> 0%
where the time goes in v1:
time: 58.3 us; the launch traced here: 58.1 us
  Pallas kernels  53 us (91%)
  local copies, waits for them, and re-layouts  4.51 us (8%)
  between operations  0.64 us (1%)
    pallas_call x1, Pallas kernels, body(): pl.pallas_call(functools.partial(kernel, n, leaf), out_shape=(jax.ShapeDt...  53 us
    unnamed x2, local copies, waits for them, and re-layouts  3.34 us
    reshape x1, local copies, waits for them, and re-layouts, body(): jnp.pad(map_pos, (0, 128 - tile)).reshape(1, 1, 128)  1.17 us

profile of v1, /device:TPU:0, one launch (start us, length us, event | category | flops | bytes accessed | tf_op | source)
XLA Modules:
  0.0 58.1 jit_solution(6036018357713417006)
XLA Ops:
  0.6 1.2 %pad_bitcast_fusion.mp_ref = f32[1,1,128]{2,1,0:T(1,128)} fusion(f32[64]{0:T(128)} %param.14), kind=kLoop, calls=%fused_computation | loop fusion | bytes 768 | tf_op jit(solution)/shard_map/reshape | solution.py:355
  1.8 53.0 %shard_map.104 = (f32[512,256]{1,0:T(8,128)}, f32[64,256]{1,0:T(8,128)}) custom-call(bf16[512,256]{1,0:T(8,128)(2,1)} %res_ref.1, bf16[512,128]{1,0:T(8,128)(2,1)} %inv_ref.1, f32[7,512,128]{2,1,0:T(8,128)} %bl_ref.1, f32[7,512,128]{2,1,0:T(8,128)} %br_ref.1, f32[32,1,512]{2,1,0:T(1,128)} %bitcast.3, f32[1,1,128]{2,1,0:T(1,128)} %pad_bitcast_fusion.mp_ref, ...), custom_call_target="tpu_custom_call" | custom-call | tf_op jit(solution)/shard_map/pallas_call | solution.py:316
  54.8 1.9 %copy.13 = f32[512,256]{1,0:T(8,128)} copy(f32[512,256]{1,0:T(8,128)} %get-tuple-element.4) | data formatting | bytes 1048576
  56.6 1.5 %copy.14 = f32[64,256]{1,0:T(8,128)} copy(f32[64,256]{1,0:T(8,128)} %get-tuple-element.5) | data formatting | bytes 131072

commit v2 on v1

--- a/solution.py
+++ b/solution.py
@@ -9,6 +9,7 @@
 
 AMPLITUDE = 0.2
 FAR = -1e6
+PIECES = 4
 f32 = jnp.float32
 bf16 = jnp.bfloat16
 
@@ -31,15 +32,17 @@
     leaf,
     res_ref,
     inv_ref,
-    bl_ref,
-    br_ref,
+    bl_hbm,
+    br_hbm,
     pp_ref,
     mp_ref,
     prior_ref,
     first_ref,
     count_ref,
-    out_ref,
+    out_hbm,
     map_ref,
+    bl_ref,
+    br_ref,
     xs,
     rth,
     rtl,
@@ -58,8 +61,16 @@
     acc,
     ms,
     mr,
+    fs,
+    fr,
+    ss,
+    sr,
+    lt,
+    lr,
     send_sem,
     recv_sem,
+    load_sem,
+    store_sem,
 ):
     rows, samples = res_ref.shape
     rank = bl_ref.shape[2]
@@ -87,6 +98,15 @@
         started.append(copy)
         return copy
 
+    order = list(range(depth)) + list(range(levels - 1, depth - 1, -1))
+    loads = {}
+    for l in order:
+        for side, (src, dst) in enumerate(((br_hbm, br_ref), (bl_hbm, bl_ref))):
+            loads[side, l] = pltpu.make_async_copy(
+                src.at[l], dst.at[l], load_sem.at[side * levels + l]
+            )
+            loads[side, l].start()
+
     barrier = pltpu.get_barrier_semaphore()
     for k in range(depth):
         pl.semaphore_signal(
@@ -94,19 +114,20 @@
         )
 
     pairs = [m * (m + 1) // 2 for m in range(depth)]
-    g_off, t_off, m_off = [], [], []
-    g_at = t_at = m_at = 0
+    g_off, t_off = [], []
+    g_at = t_at = 0
     for k in range(depth):
         m = depth - 1 - k
         g_off.append(g_at)
         t_off.append(t_at)
-        m_off.append(m_at)
         g_at += pairs[m]
         t_at += m + 1
-        m_at += n // 2 ** (k + 1) * tile
-
-    mpb[0] = mp_ref[0]
+
+    mpb[0] = jnp.zeros((1, 128), f32)
+    mpb[0, :, :tile] = mp_ref[0]
     for l in range(depth):
+        loads[0, l].wait()
+        loads[1, l].wait()
         high, low = split(br_ref[l].T)
         rth[l * rank : (l + 1) * rank, :] = high
         rtl[l * rank : (l + 1) * rank, :] = low
@@ -131,13 +152,28 @@
     def start_mp(k):
         return remote(mpb.at[pl.ds(0, 2**k)], mpb.at[pl.ds(2**k, 2**k)], k)
 
+    g_copy = start_g(0) if depth > 1 else None
     mp_copy = start_mp(0)
-    g_copy = start_g(0) if depth > 1 else None
+
+    def next_g(k):
+        m = depth - 1 - k
+        rest = pairs[m] - m
+        if rest <= 0:
+            return None
+        total = gf[g_off[k] + m : g_off[k] + pairs[m]] + gr[
+            g_off[k] + m : g_off[k] + pairs[m]
+        ].astype(f32)
+        gf[g_off[k + 1] : g_off[k + 1] + rest] = total
+        gs[g_off[k + 1] : g_off[k + 1] + rest] = total.astype(bf16)
+        return start_g(k + 1)
 
     for b in range(rows // leaf):
         part = mm(inv_ref[b * leaf : (b + 1) * leaf, :], res_ref[b * leaf : (b + 1) * leaf, :])
         xs[b * leaf : (b + 1) * leaf, :] = part
     total_rows = rows * n
+    for level in range(levels - 1, depth - 1, -1):
+        loads[0, level].wait()
+        loads[1, level].wait()
     for level in range(levels - 1, depth - 1, -1):
         size = total_rows // 2 ** (level + 1)
         count = rows // size
@@ -149,17 +185,20 @@
             view = slice(a * size, (a + 1) * size)
             xs[view, :] += mm3(split(bl_ref[level, view, :]), projected[a ^ 1])
 
+    if depth > 1:
+        g_copy.wait_recv()
+        g_copy = next_g(0)
     mp_copy.wait_recv()
     mp_next = 1
     if mp_next < depth:
         mp_copy = start_mp(mp_next)
 
+    x_high, x_low = split(xs[...])
+    t_all = mm(rth[...], x_high) + mm(rth[...], x_low) + mm(rtl[...], x_high)
     for h in range(2):
-        x_high, x_low = split(xs[:, h * half : (h + 1) * half])
-        t_all = mm(rth[...], x_high) + mm(rth[...], x_low) + mm(rtl[...], x_high)
-        t_all = t_all.reshape(depth, rank, half)
-        tf[h] = t_all
-        ts[h, pl.ds(0, depth)] = t_all.astype(bf16)
+        t_half = t_all[:, h * half : (h + 1) * half].reshape(depth, rank, half)
+        tf[h] = t_half
+        ts[h, pl.ds(0, depth)] = t_half.astype(bf16)
 
     own_u = pp_ref[me]
 
@@ -204,16 +243,9 @@
             mp_next += 1
             if mp_next < depth:
                 mp_copy = start_mp(mp_next)
-        if m > 0:
+        if k > 0 and m > 0:
             g_copy.wait_recv()
-            rest = pairs[m] - m
-            if rest > 0:
-                total = gf[g_off[k] + m : g_off[k] + pairs[m]] + gr[
-                    g_off[k] + m : g_off[k] + pairs[m]
-                ].astype(f32)
-                gf[g_off[k + 1] : g_off[k + 1] + rest] = total
-                gs[g_off[k + 1] : g_off[k + 1] + rest] = total.astype(bf16)
-                g_copy = start_g(k + 1)
+            g_copy = next_g(k)
         if k == depth - 2:
             while mp_next < depth:
                 mp_copy.wait_recv()
@@ -247,7 +279,7 @@
     def finish(columns, parts):
         stacked = jnp.concatenate(parts, axis=0)
         total = xs[:, columns] + mm(lh[...], stacked) + mm(ll[...], stacked)
-        out_ref[:, columns] = total
+        xs[:, columns] = total
         co[:, columns] = total.astype(bf16)
 
     finish(mine_cols, [tr[t_off[depth - 1 - m] + m] for m in range(depth)])
@@ -255,39 +287,90 @@
         copy.wait_recv()
     finish(other_cols, [cbuf[m, 1 - par] for m in range(depth)])
 
-    step_rows = min(256, n // 2 * tile)
-    half_rows = n // 2 * tile
-
-    def send_part(i, carry):
-        at = pl.multiple_of(i * step_rows, step_rows)
-        ms[pl.ds(at, step_rows), :] = mm(
-            wts[pl.ds(half_rows + at, step_rows), :], co[...]
-        ).astype(bf16)
-        return carry
-
-    def keep_part(i, carry):
-        at = pl.multiple_of(i * step_rows, step_rows)
-        acc[pl.ds(at, step_rows), :] = mm(wts[pl.ds(at, step_rows), :], co[...])
-        return carry
-
-    lax.fori_loop(0, half_rows // step_rows, send_part, 0)
-    copy = remote(ms.at[pl.ds(0, half_rows)], mr.at[pl.ds(0, half_rows)], 0)
-    lax.fori_loop(0, half_rows // step_rows, keep_part, 0)
-    for k in range(1, depth):
-        size = n // 2 ** (k + 1) * tile
+    store = pltpu.make_async_copy(xs, out_hbm, store_sem.at[0])
+    store.start()
+
+    quarter = n // 8 * tile
+    half_rows = 4 * quarter
+    first_copies = {}
+    for j in (3, 2, 1, 0):
+        low = half_rows + j * quarter
+        ms[j] = mm(wts[low : low + quarter, :], co[...]).astype(bf16)
+        first_copies[j] = remote(ms.at[j], mr.at[j], 0)
+
+    def keep(j):
+        part = mm(wts[j * quarter : (j + 1) * quarter, :], co[...])
+        for c in range(2):
+            acc[c, j] = part[:, c * half : (c + 1) * half]
+
+    def summed(c, j):
+        return acc[c, j] + mr[j, :, c * half : (c + 1) * half].astype(f32)
+
+    keep(3)
+    keep(2)
+    first_copies[3].wait_recv()
+    first_copies[2].wait_recv()
+    fs[0, 0] = summed(0, 2).astype(bf16)
+    fs[0, 1] = summed(0, 3).astype(bf16)
+    copy_a = remote(fs.at[0], fr.at[0], 1)
+    keep(1)
+    first_copies[1].wait_recv()
+    fs[1, 0] = summed(1, 1).astype(bf16)
+    fs[1, 1] = summed(1, 3).astype(bf16)
+    copy_b = remote(fs.at[1], fr.at[1], 2)
+    keep(0)
+    first_copies[0].wait_recv()
+    acc[0, 1] = summed(0, 1)
+    acc[1, 2] = summed(1, 2)
+    acc[0, 0] = summed(0, 0)
+    acc[1, 0] = summed(1, 0)
+    copy_a.wait_recv()
+    ss[0] = (acc[0, 1] + fr[0, 1].astype(f32)).astype(bf16)
+    copy_a = remote(ss.at[0], sr.at[0], 2)
+    copy_b.wait_recv()
+    ss[1] = (acc[1, 2] + fr[1, 1].astype(f32)).astype(bf16)
+    copy_b = remote(ss.at[1], sr.at[1], 1)
+    sums = [acc[c, 0] + fr[c, 0].astype(f32) for c in range(2)]
+    copy_a.wait_recv()
+    copy_b.wait_recv()
+    size = quarter
+    for c in range(2):
+        acc[c, 0] = sums[c] + sr[c].astype(f32)
+    base = 0
+    for k in range(3, depth):
+        size = size // 2
+        for c in range(2):
+            lt[c, base : base + size, :] = acc[c, 0, size : 2 * size, :].astype(bf16)
+        copy = remote(
+            lt.at[:, pl.ds(base, size)], lr.at[:, pl.ds(base, size)], k
+        )
         copy.wait_recv()
-        old = m_off[k - 1]
-        ms[m_off[k] : m_off[k] + size, :] = (
-            acc[size : 2 * size, :] + mr[old + size : old + 2 * size, :].astype(f32)
-        ).astype(bf16)
-        copy = remote(ms.at[pl.ds(m_off[k], size)], mr.at[pl.ds(m_off[k], size)], k)
-        acc[:size, :] += mr[old : old + size, :].astype(f32)
-    partial = prior_ref[...].astype(f32) + acc[:tile, :]
-    copy.wait_recv()
-    old = m_off[depth - 1]
-    map_ref[...] = partial + mr[old : old + tile, :].astype(f32)
+        for c in range(2):
+            acc[c, 0, :size, :] += lr[c, base : base + size, :].astype(f32)
+        base += size
+    for c in range(2):
+        cols = slice(c * half, (c + 1) * half)
+        map_ref[:, cols] = prior_ref[:, cols].astype(f32) + acc[c, 0, :tile, :]
+    store.wait()
     for copy in started:
         copy.wait_send()
+
+
+def deliver(solved_ref, mapped_ref, out_ref, map_ref, held, spots, in_sem, out_sem):
+    piece = held.shape[0] // PIECES
+    moves = [(mapped_ref, spots, map_ref)]
+    for i in range(PIECES):
+        view = pl.ds(i * piece, piece)
+        moves.append((solved_ref.at[view], held.at[view], out_ref.at[view]))
+    reads = [pltpu.make_async_copy(a, b, in_sem.at[i]) for i, (a, b, _) in enumerate(moves)]
+    writes = [pltpu.make_async_copy(b, c, out_sem.at[i]) for i, (_, b, c) in enumerate(moves)]
+    for read in reads:
+        read.start()
+    for read, write in zip(reads, writes):
+        read.wait()
+        write.start()
+    for write in writes:
+        write.wait()
 
 
 def body(
@@ -312,16 +395,20 @@
     t_total = depth * (depth + 1) // 2
     vmem = pl.BlockSpec(memory_space=pltpu.VMEM)
     smem = pl.BlockSpec(memory_space=pltpu.SMEM)
-    copies = 5 * depth
-    return pl.pallas_call(
+    anywhere = pl.BlockSpec(memory_space=pl.ANY)
+    copies = 5 * depth + 8
+    quarter = n // 8 * tile
+    solved, mapped = pl.pallas_call(
         functools.partial(kernel, n, leaf),
         out_shape=(
             jax.ShapeDtypeStruct((rows, samples), f32),
             jax.ShapeDtypeStruct((tile, samples), f32),
         ),
-        in_specs=[vmem] * 7 + [smem] * 2,
-        out_specs=(vmem, vmem),
+        in_specs=[vmem] * 2 + [anywhere] * 2 + [vmem] * 3 + [smem] * 2,
+        out_specs=(anywhere, vmem),
         scratch_shapes=[
+            pltpu.VMEM((levels, rows, rank), f32),
+            pltpu.VMEM((levels, rows, rank), f32),
             pltpu.VMEM((rows, samples), f32),
             pltpu.VMEM((depth * rank, rows), bf16),
             pltpu.VMEM((depth * rank, rows), bf16),
@@ -337,11 +424,19 @@
             pltpu.VMEM((rows, samples), bf16),
             pltpu.VMEM((n, 1, 128), f32),
             pltpu.VMEM((n * tile, rows), bf16),
-            pltpu.VMEM((n // 2 * tile, samples), f32),
-            pltpu.VMEM((n * tile, samples), bf16),
-            pltpu.VMEM((n * tile, samples), bf16),
+            pltpu.VMEM((2, 4, quarter, half), f32),
+            pltpu.VMEM((4, quarter, samples), bf16),
+            pltpu.VMEM((4, quarter, samples), bf16),
+            pltpu.VMEM((2, 2, quarter, half), bf16),
+            pltpu.VMEM((2, 2, quarter, half), bf16),
+            pltpu.VMEM((2, quarter, half), bf16),
+            pltpu.VMEM((2, quarter, half), bf16),
+            pltpu.VMEM((2, quarter, half), bf16),
+            pltpu.VMEM((2, quarter, half), bf16),
             pltpu.SemaphoreType.DMA((copies,)),
             pltpu.SemaphoreType.DMA((copies,)),
+            pltpu.SemaphoreType.DMA((2 * levels,)),
+            pltpu.SemaphoreType.DMA((1,)),
         ],
         compiler_params=pltpu.CompilerParams(
             collective_id=0, has_side_effects=True, vmem_limit_bytes=60 * 1024 * 1024
@@ -352,11 +447,26 @@
         basis_left,
         basis_right,
         point_pos.reshape(n, 1, rows),
-        jnp.pad(map_pos, (0, 128 - tile)).reshape(1, 1, 128),
+        map_pos.reshape(1, 1, tile),
         prior_map,
         block_first,
         block_count,
     )
+    return pl.pallas_call(
+        deliver,
+        out_shape=(
+            jax.ShapeDtypeStruct((rows, samples), f32),
+            jax.ShapeDtypeStruct((tile, samples), f32),
+        ),
+        in_specs=[anywhere] * 2,
+        out_specs=(anywhere, anywhere),
+        scratch_shapes=[
+            pltpu.VMEM((rows, samples), f32),
+            pltpu.VMEM((tile, samples), f32),
+            pltpu.SemaphoreType.DMA((PIECES + 1,)),
+            pltpu.SemaphoreType.DMA((PIECES + 1,)),
+        ],
+    )(solved, mapped)
 
 
 def solution(mesh):

time: 58.3 us -> 51.7 us (0.89)
  local copies, waits for them, and re-layouts: 4.51 us -> 0 us
  Pallas kernels: 53 us -> 50.8 us
    pallas_call x1, Pallas kernels: 53 us -> 49 us  [body(): pl.pallas_call(functools.partial(kernel, n, leaf), out_shape=(jax.ShapeDt...]
    unnamed x2 -> x0, local copies, waits for them, and re-layouts: 3.34 us -> none
    pallas_call x0 -> x1, Pallas kernels: none -> 1.87 us  [body(): pl.pallas_call(deliver, out_shape=(jax.ShapeDtypeStruct((rows, samples),...]
    reshape x1 -> x0, local copies, waits for them, and re-layouts: 1.17 us -> none  [body(): jnp.pad(map_pos, (0, 128 - tile)).reshape(1, 1, 128)]
where the time goes in v2:
time: 51.7 us; the launch traced here: 51.5 us
  Pallas kernels  50.8 us (98%)
  between operations  0.64 us (1%)
    pallas_call x1, Pallas kernels, body(): pl.pallas_call(functools.partial(kernel, n, leaf), out_shape=(jax.ShapeDt...  49 us
    pallas_call x1, Pallas kernels, body(): pl.pallas_call(deliver, out_shape=(jax.ShapeDtypeStruct((rows, samples),...  1.87 us

profile of v2, /device:TPU:0, one launch (start us, length us, event | category | flops | bytes accessed | tf_op | source)
XLA Modules:
  0.0 51.5 jit_solution(5914834383900854957)
XLA Ops:
  0.6 49.0 %shard_map.104 = (f32[512,256]{1,0:T(8,128)}, f32[64,256]{1,0:T(8,128)}) custom-call(bf16[512,256]{1,0:T(8,128)(2,1)} %res_ref.1, bf16[512,128]{1,0:T(8,128)(2,1)} %inv_ref.1, f32[7,512,128]{2,1,0:T(8,128)} %bl_hbm.1, f32[7,512,128]{2,1,0:T(8,128)} %br_hbm.1, f32[32,1,512]{2,1,0:T(1,128)} %bitcast.2, f32[1,1,64]{2,1,0:T(1,128)} %bitcast.3, ...), custom_call_target="tpu_custom_call" | custom-call | tf_op jit(solution)/shard_map/pallas_call | solution.py:401
  49.6 1.9 %shard_map.105 = (f32[512,256]{1,0:T(8,128)}, f32[64,256]{1,0:T(8,128)}) custom-call(f32[512,256]{1,0:T(8,128)} %get-tuple-element.4.solved_ref, f32[64,256]{1,0:T(8,128)} %get-tuple-element.5.mapped_ref), custom_call_target="tpu_custom_call" | custom-call | tf_op jit(solution)/shard_map/pallas_call | solution.py:455

commit v3 on v2

--- a/solution.py
+++ b/solution.py
@@ -10,6 +10,7 @@
 AMPLITUDE = 0.2
 FAR = -1e6
 PIECES = 4
+TOGETHER = 4
 f32 = jnp.float32
 bf16 = jnp.bfloat16
 
@@ -203,7 +204,7 @@
     own_u = pp_ref[me]
 
     def weights(low_e, high_e):
-        def one(e, carry):
+        def one(e):
             spot = 0
             other = 0
             for i in range(depth):
@@ -223,9 +224,13 @@
                 square = rest * rest
                 value = AMPLITUDE * (square * square * (1.0 + 4.0 * scaled))
                 wts[pl.ds(base, tile), b * leaf : (b + 1) * leaf] = value.astype(bf16)
+
+        def several(i, carry):
+            for j in range(TOGETHER):
+                one(low_e + i * TOGETHER + j)
             return carry
 
-        lax.fori_loop(low_e, high_e, one, 0)
+        lax.fori_loop(0, (high_e - low_e) // TOGETHER, several, 0)
 
     forwards = []
     for k in range(depth):
@@ -252,9 +257,9 @@
                 mp_next += 1
                 if mp_next < depth:
                     mp_copy = start_mp(mp_next)
-            weights(0, n // 2)
-        if k == depth - 1:
-            weights(n // 2, n)
+        late = k - (depth - 4)
+        if late >= 0:
+            weights(late * (n // 4), (late + 1) * (n // 4))
         for copy in t_copies:
             copy.wait_recv()
         if k > 0:

time: 51.7 us -> 51.4 us (level)
  no operation moved by 1% of the time
where the time goes in v3:
time: 51.4 us; the launch traced here: 51.2 us
  Pallas kernels  50.5 us (98%)
  between operations  0.64 us (1%)
    pallas_call x1, Pallas kernels, body(): pl.pallas_call(functools.partial(kernel, n, leaf), out_shape=(jax.ShapeDt...  48.6 us
    pallas_call x1, Pallas kernels, body(): pl.pallas_call(deliver, out_shape=(jax.ShapeDtypeStruct((rows, samples),...  1.87 us

profile of v3, /device:TPU:0, one launch (start us, length us, event | category | flops | bytes accessed | tf_op | source)
XLA Modules:
  0.0 51.2 jit_solution(4358280965043011129)
XLA Ops:
  0.6 48.6 %shard_map.104 = (f32[512,256]{1,0:T(8,128)}, f32[64,256]{1,0:T(8,128)}) custom-call(bf16[512,256]{1,0:T(8,128)(2,1)} %res_ref.1, bf16[512,128]{1,0:T(8,128)(2,1)} %inv_ref.1, f32[7,512,128]{2,1,0:T(8,128)} %bl_hbm.1, f32[7,512,128]{2,1,0:T(8,128)} %br_hbm.1, f32[32,1,512]{2,1,0:T(1,128)} %bitcast.2, f32[1,1,64]{2,1,0:T(1,128)} %bitcast.3, ...), custom_call_target="tpu_custom_call" | custom-call | tf_op jit(solution)/shard_map/pallas_call | solution.py:406
  49.3 1.9 %shard_map.105 = (f32[512,256]{1,0:T(8,128)}, f32[64,256]{1,0:T(8,128)}) custom-call(f32[512,256]{1,0:T(8,128)} %get-tuple-element.4.solved_ref, f32[64,256]{1,0:T(8,128)} %get-tuple-element.5.mapped_ref), custom_call_target="tpu_custom_call" | custom-call | tf_op jit(solution)/shard_map/pallas_call | solution.py:460

commit v4 on v3

--- a/solution.py
+++ b/solution.py
@@ -146,14 +146,20 @@
     pl.semaphore_wait(barrier, depth)
 
     def start_g(k):
-        size = pairs[depth - 1 - k]
-        view = pl.ds(g_off[k], size)
-        return remote(gs.at[view], gr.at[view], k)
+        m = depth - 1 - k
+        rest = pairs[m] - m
+        copies = []
+        if rest > 0:
+            view = pl.ds(g_off[k] + m, rest)
+            copies.append(remote(gs.at[view], gr.at[view], k))
+        view = pl.ds(g_off[k], m)
+        copies.append(remote(gs.at[view], gr.at[view], k))
+        return copies
 
     def start_mp(k):
         return remote(mpb.at[pl.ds(0, 2**k)], mpb.at[pl.ds(2**k, 2**k)], k)
 
-    g_copy = start_g(0) if depth > 1 else None
+    g_heads = {0: start_g(0)} if depth > 1 else {}
     mp_copy = start_mp(0)
 
     def next_g(k):
@@ -161,12 +167,14 @@
         rest = pairs[m] - m
         if rest <= 0:
             return None
+        g_heads[k][0].wait_recv()
         total = gf[g_off[k] + m : g_off[k] + pairs[m]] + gr[
             g_off[k] + m : g_off[k] + pairs[m]
         ].astype(f32)
         gf[g_off[k + 1] : g_off[k + 1] + rest] = total
         gs[g_off[k + 1] : g_off[k + 1] + rest] = total.astype(bf16)
-        return start_g(k + 1)
+        g_heads[k + 1] = start_g(k + 1)
+        return None
 
     for b in range(rows // leaf):
         part = mm(inv_ref[b * leaf : (b + 1) * leaf, :], res_ref[b * leaf : (b + 1) * leaf, :])
@@ -187,8 +195,7 @@
             xs[view, :] += mm3(split(bl_ref[level, view, :]), projected[a ^ 1])
 
     if depth > 1:
-        g_copy.wait_recv()
-        g_copy = next_g(0)
+        next_g(0)
     mp_copy.wait_recv()
     mp_next = 1
     if mp_next < depth:
@@ -249,8 +256,7 @@
             if mp_next < depth:
                 mp_copy = start_mp(mp_next)
         if k > 0 and m > 0:
-            g_copy.wait_recv()
-            g_copy = next_g(k)
+            next_g(k)
         if k == depth - 2:
             while mp_next < depth:
                 mp_copy.wait_recv()
@@ -265,6 +271,7 @@
         if k > 0:
             forwards.append(remote(tr.at[t_off[k] + m], cbuf.at[m, par], 0))
         if m > 0:
+            g_heads[k][-1].wait_recv()
             mine = ts[par, t_off[k] + m]
             theirs = tr[t_off[k] + m]
             g_mine = gs[g_off[k] : g_off[k] + m].reshape(m * rank, rank)
@@ -401,7 +408,7 @@
     vmem = pl.BlockSpec(memory_space=pltpu.VMEM)
     smem = pl.BlockSpec(memory_space=pltpu.SMEM)
     anywhere = pl.BlockSpec(memory_space=pl.ANY)
-    copies = 5 * depth + 8
+    copies = 6 * depth + 8
     quarter = n // 8 * tile
     solved, mapped = pl.pallas_call(
         functools.partial(kernel, n, leaf),

time: 51.4 us -> 51.3 us (level)
  no operation moved by 1% of the time
where the time goes in v4:
time: 51.3 us; the launch traced here: 51.1 us
  Pallas kernels  50.4 us (98%)
  between operations  0.64 us (1%)
    pallas_call x1, Pallas kernels, body(): pl.pallas_call(functools.partial(kernel, n, leaf), out_shape=(jax.ShapeDt...  48.6 us
    pallas_call x1, Pallas kernels, body(): pl.pallas_call(deliver, out_shape=(jax.ShapeDtypeStruct((rows, samples),...  1.87 us

profile of v4, /device:TPU:0, one launch (start us, length us, event | category | flops | bytes accessed | tf_op | source)
XLA Modules:
  0.0 51.1 jit_solution(9745763483166147892)
XLA Ops:
  0.6 48.6 %shard_map.104 = (f32[512,256]{1,0:T(8,128)}, f32[64,256]{1,0:T(8,128)}) custom-call(bf16[512,256]{1,0:T(8,128)(2,1)} %res_ref.1, bf16[512,128]{1,0:T(8,128)(2,1)} %inv_ref.1, f32[7,512,128]{2,1,0:T(8,128)} %bl_hbm.1, f32[7,512,128]{2,1,0:T(8,128)} %br_hbm.1, f32[32,1,512]{2,1,0:T(1,128)} %bitcast.2, f32[1,1,64]{2,1,0:T(1,128)} %bitcast.3, ...), custom_call_target="tpu_custom_call" | custom-call | tf_op jit(solution)/shard_map/pallas_call | solution.py:413
  49.2 1.9 %shard_map.105 = (f32[512,256]{1,0:T(8,128)}, f32[64,256]{1,0:T(8,128)}) custom-call(f32[512,256]{1,0:T(8,128)} %get-tuple-element.4.solved_ref, f32[64,256]{1,0:T(8,128)} %get-tuple-element.5.mapped_ref), custom_call_target="tpu_custom_call" | custom-call | tf_op jit(solution)/shard_map/pallas_call | solution.py:467
